TPU v7x, 256 devices: a whole 4x4x8 slice. The times are simulated.
256 devices in a mesh: row: 32 (over y_hi, z, core), col: 8 (over y_lo, x).
Axes of the slice: x: 4, y: 4 (y_hi: 2, y_lo: 2; y = y_hi * 2 + y_lo), z: 8, core: 2. Of those that a mesh axis runs over, the one named last changes fastest.
Arguments:
- features: bfloat16 [128, 32768], P(None, ('row', 'col')), may hold values from -6 to 6
- positions: float32 [3, 32768], P(None, ('row', 'col')), may hold values from 0 to 6
- tile_pairs: int32 [32, 8, 2, 4], P('row', 'col'), may hold values from 0 to 31, as said below
- pair_count: int32 [32, 8], P('row', 'col'), may hold values from 1 to 4, as said below
- masks: int32 [32, 8, 4, 128, 128], P('row', 'col'), may hold values 0 or 1
- w_in: bfloat16 [128, 128], replicated, may hold values from -0.5 to 0.5
- w_f1: bfloat16 [64, 128], replicated, may hold values from -3 to 3
- b_f1: float32 [128], replicated, may hold values from -3 to 3
- w_f2: bfloat16 [128, 128], replicated, may hold values from -0.1875 to 0.1875
- b_f2: float32 [128], replicated, may hold values from -2 to 2
- w_o1: bfloat16 [128, 128], replicated, may hold values from -0.25 to 0.25
- b_o1: float32 [128], replicated, may hold values from -3 to 3
- w_o2: bfloat16 [128, 128], replicated, may hold values from -0.5 to 0.5
- b_o2: float32 [128], replicated, may hold values from -3 to 3
- read_w: float32 [128], replicated, may hold values from -2 to 2
Outputs:
- features_out: bfloat16 [128, 32768], P(None, ('row', 'col'))
- forces: float32 [3, 32768], P(None, ('row', 'col'))
Inputs may be any that keep to these rules, and one draw needn't show every extreme that they name: Only slots 0 to pair_count[r, c] - 1 of tile_pairs and masks of block (r, c) are listed. tile_pairs[r, c, 0, s] is a receiver tile below 8, tile_pairs[r, c, 1, s] a sender tile below 32; the slots of one grid block hold distinct tile pairs.
All inputs are finite; a program needn't handle non-finite values. No bound on the sum of `masks` on one device may be relied on, other than what follows from the above.
Results may differ from a plain program's by a relative error of at most 0.0075.
Values may be sent and summed in bfloat16 or wider, within the bound.
A program may use at most 64 MiB of HBM per device.

v0:
```python
import math

import jax
import jax.numpy as jnp
from jax import lax
from jax.sharding import PartitionSpec as P

SOFTENING = 0.25
GAMMA_RBF = 10.0
CENTER_MAX = 10.0
CUTOFF = 12.0


def shifted_softplus(value):
    return jax.nn.softplus(value) - math.log(2.0)


def filter_forward(distance, w_f1, b_f1, w_f2, b_f2):
    nbasis = w_f1.shape[0]
    centers = (jnp.arange(nbasis, dtype=jnp.float32) * (CENTER_MAX / (nbasis - 1)))[:, None, None]
    offset = distance[None] - centers
    gauss = jnp.exp(-GAMMA_RBF * offset * offset)
    basis = gauss.astype(jnp.bfloat16)
    hidden_pre = (
        jnp.einsum("kh,krc->hrc", w_f1, basis, preferred_element_type=jnp.float32)
        + b_f1[:, None, None]
    )
    hidden = shifted_softplus(hidden_pre).astype(jnp.bfloat16)
    filter_base = (
        jnp.einsum("hf,hrc->frc", w_f2, hidden, preferred_element_type=jnp.float32)
        + b_f2[:, None, None]
    )
    cutoff = 0.5 * (jnp.cos(math.pi / CUTOFF * distance) + 1.0)
    return (offset, gauss, hidden_pre, filter_base, cutoff)


def pair_geometry(pos_rows, pos_cols):
    separation = pos_rows[:, :, None] - pos_cols[:, None, :]
    distance = jnp.sqrt(jnp.sum(separation * separation, axis=0) + SOFTENING)
    return (separation, distance)


def tile_messages(pos_rows, pos_cols, sender_feats, pair_mask, params):
    separation, distance = pair_geometry(pos_rows, pos_cols)
    offset, gauss, hidden_pre, filter_base, cutoff = filter_forward(distance, *params)
    weighted = filter_base * (cutoff * pair_mask)[None]
    return jnp.sum(weighted * sender_feats.astype(jnp.float32)[:, None, :], axis=2)


def tile_forces(pos_rows, pos_cols, sender_feats, grad_rows, pair_mask, params):
    w_f1, b_f1, w_f2, b_f2 = params
    separation, distance = pair_geometry(pos_rows, pos_cols)
    offset, gauss, hidden_pre, filter_base, cutoff = filter_forward(distance, *params)
    pair_grad = (
        grad_rows[:, :, None] * sender_feats.astype(jnp.float32)[:, None, :] * pair_mask[None]
    )
    filter_grad = (pair_grad * cutoff[None]).astype(jnp.bfloat16)
    cutoff_grad = jnp.sum(pair_grad * filter_base, axis=0)
    hidden_grad = jnp.einsum("hf,frc->hrc", w_f2, filter_grad, preferred_element_type=jnp.float32)
    hidden_grad = (hidden_grad * jax.nn.sigmoid(hidden_pre)).astype(jnp.bfloat16)
    basis_grad = jnp.einsum("kh,hrc->krc", w_f1, hidden_grad, preferred_element_type=jnp.float32)
    dist_grad = -2.0 * GAMMA_RBF * jnp.sum(basis_grad * gauss * offset, axis=0)
    dist_grad = (
        dist_grad - 0.5 * math.pi / CUTOFF * jnp.sin(math.pi / CUTOFF * distance) * cutoff_grad
    )
    push = separation * (dist_grad / distance)[None]
    return (-jnp.sum(push, axis=2), jnp.sum(push, axis=1))


def atom_update(messages, w_o1, b_o1, w_o2, b_o2, read_w):
    pre_act = (
        jnp.einsum(
            "fo,fa->oa", w_o1, messages.astype(jnp.bfloat16), preferred_element_type=jnp.float32
        )
        + b_o1[:, None]
    )
    activated = shifted_softplus(pre_act).astype(jnp.bfloat16)
    update = (
        jnp.einsum("fo,fa->oa", w_o2, activated, preferred_element_type=jnp.float32) + b_o2[:, None]
    )
    direction = jnp.dot(w_o2.astype(jnp.float32), read_w, precision=lax.Precision.HIGHEST)
    message_grad = jnp.dot(
        w_o1.astype(jnp.float32),
        direction[:, None] * jax.nn.sigmoid(pre_act),
        precision=lax.Precision.HIGHEST,
    )
    return (update, message_grad)


def local(
    features,
    positions,
    tile_pairs,
    pair_count,
    masks,
    w_in,
    w_f1,
    b_f1,
    w_f2,
    b_f2,
    w_o1,
    b_o1,
    w_o2,
    b_o2,
    read_w,
):
    params = (w_f1, b_f1, w_f2, b_f2)
    owned = features.shape[1]
    tile = masks.shape[-1]
    row_count = lax.axis_size("row")
    col_count = lax.axis_size("col")
    row_index = lax.axis_index("row")
    col_index = lax.axis_index("col")
    row_span = col_count * owned
    projected = jnp.einsum("fo,fa->oa", w_in, features, preferred_element_type=jnp.float32).astype(
        jnp.bfloat16
    )
    sender_block = lax.all_gather(projected, "row", axis=1, tiled=True)
    every_position = lax.all_gather(positions, ("row", "col"), axis=1, tiled=True)
    row_positions = lax.dynamic_slice_in_dim(every_position, row_index * row_span, row_span, 1)
    col_positions = lax.dynamic_index_in_dim(
        every_position.reshape(3, row_count, col_count, owned), col_index, 2, keepdims=False
    )
    col_positions = col_positions.reshape(3, row_count * owned)
    slot_pairs = tile_pairs[0, 0]
    slot_masks = masks[0, 0]
    pair_total = pair_count[0, 0]

    def locate(slot_index):
        row_start = slot_pairs[0, slot_index] * tile
        col_start = slot_pairs[1, slot_index] * tile
        pair_mask = lax.dynamic_index_in_dim(slot_masks, slot_index, 0, keepdims=False).astype(
            jnp.float32
        )
        return (row_start, col_start, pair_mask)

    def forward_slot(slot_index, totals):
        row_start, col_start, pair_mask = locate(slot_index)
        tile_sum = tile_messages(
            lax.dynamic_slice_in_dim(row_positions, row_start, tile, 1),
            lax.dynamic_slice_in_dim(col_positions, col_start, tile, 1),
            lax.dynamic_slice_in_dim(sender_block, col_start, tile, 1),
            pair_mask,
            params,
        )
        current = lax.dynamic_slice_in_dim(totals, row_start, tile, 1)
        return lax.dynamic_update_slice_in_dim(totals, current + tile_sum, row_start, 1)

    partial_messages = lax.fori_loop(
        jnp.int32(0),
        pair_total,
        forward_slot,
        jnp.zeros((projected.shape[0], row_span), jnp.float32),
    )
    block_messages_sum = lax.psum(partial_messages, "col")
    block_update, message_grad = atom_update(block_messages_sum, w_o1, b_o1, w_o2, b_o2, read_w)
    update = lax.dynamic_slice_in_dim(block_update, col_index * owned, owned, 1)
    features_out = (features.astype(jnp.float32) + update).astype(jnp.bfloat16)

    def backward_slot(slot_index, carried):
        row_force, col_force = carried
        row_start, col_start, pair_mask = locate(slot_index)
        row_part, col_part = tile_forces(
            lax.dynamic_slice_in_dim(row_positions, row_start, tile, 1),
            lax.dynamic_slice_in_dim(col_positions, col_start, tile, 1),
            lax.dynamic_slice_in_dim(sender_block, col_start, tile, 1),
            lax.dynamic_slice_in_dim(message_grad, row_start, tile, 1),
            pair_mask,
            params,
        )
        current = lax.dynamic_slice_in_dim(row_force, row_start, tile, 1)
        row_force = lax.dynamic_update_slice_in_dim(row_force, current + row_part, row_start, 1)
        current = lax.dynamic_slice_in_dim(col_force, col_start, tile, 1)
        col_force = lax.dynamic_update_slice_in_dim(col_force, current + col_part, col_start, 1)
        return (row_force, col_force)

    row_force, col_force = lax.fori_loop(
        jnp.int32(0),
        pair_total,
        backward_slot,
        (jnp.zeros((3, row_span), jnp.float32), jnp.zeros((3, row_count * owned), jnp.float32)),
    )
    receiver_side = lax.psum_scatter(row_force, "col", scatter_dimension=1, tiled=True)
    sender_side = lax.psum_scatter(col_force, "row", scatter_dimension=1, tiled=True)
    return (features_out, receiver_side + sender_side)


def solution(mesh):
    in_specs = (
        P(None, ("row", "col")),
        P(None, ("row", "col")),
        P("row", "col", None, None),
        P("row", "col"),
        P("row", "col", None, None, None),
        P(),
        P(),
        P(),
        P(),
        P(),
        P(),
        P(),
        P(),
        P(),
        P(),
    )
    out_specs = (P(None, ("row", "col")), P(None, ("row", "col")))
    return jax.shard_map(local, mesh=mesh, in_specs=in_specs, out_specs=out_specs, check_vma=False)
```

profile of v0, /device:TPU:1, one launch (start us, length us, event | category | flops | bytes accessed | tf_op | source)
XLA Modules:
  0.0 1009.7 jit_solution(12638544136404757485)
XLA Ops:
  7.2 1.6 convolution_convert_fusion
  8.9 1.5 copy.45
  10.3 0.9 copy.48
  11.2 616.7 %all_gather.6 = f32[3,32768]{1,0:T(4,128)S(1)} all-gather(f32[3,128]{1,0:T(4,128)} %param.20), channel_id=1, replica_groups=mesh['row'=32,'col'=8] {'row','col'}, dimensions={1}, use_global_device_ids=true | all-gather | bytes 394752 | tf_op jit(solution)/shard_map/all_gather | solution.py:119
  628.0 0.9 convolution_bitcast_fusion.1
  629.0 28.9 %while.26 = (s32[]{:T(128)}, f32[128,1024]{0,1:T(8,128)S(1)}, s32[]{:T(128)}, s32[2,4]{1,0:T(2,128)}, f32[3,1024]{1,0:T(4,128)S(1)}, /*index=5*/f32[3,4096]{1,0:...) while((s32[]{:T(128)}, f32[128,1024]{0,1:T(8,128)S(1)}, ...), condition=%wide.region_3.4_spmd, body=%wide.region_0.3_spmd.sunk | while | flops 837025856 | bytes 1141587 | solution.py:149
  629.7 1.4 constant_dynamic-slice_fusion.21
  632.5 0.8 constant_dynamic-slice_fusion.22
  633.4 0.1 multiply_reduce_fusion.2
  633.5 1.1 fusion.130
  634.7 8.5 fusion.131
  643.8 1.4 constant_dynamic-slice_fusion.21
  646.6 0.8 constant_dynamic-slice_fusion.22
  647.5 0.1 multiply_reduce_fusion.2
  647.7 1.1 fusion.130
  648.8 8.5 fusion.131
  658.0 29.3 %all-reduce.1 = bf16[128,1024]{0,1:T(8,128)(2,1)S(1)} all-reduce(f32[128,1024]{0,1:T(8,128)S(1)} %get-tuple-element.331), channel_id=1, replica_groups=mesh['row'=32,'col'=8] {'col'}, use_global_device_ids=true, to_apply=%region_4.5 | all-reduce | flops 131072 | bytes 786432 | tf_op jit(solution)/shard_map/psum | solution.py:155
  687.3 0.2 fusion.81
  687.5 0.5 convolution_bitcast_fusion
  688.0 60.7 %while.27 = (s32[]{:T(128)}, f32[3,1024]{1,0:T(4,128)S(1)}, f32[3,4096]{1,0:T(4,128)S(1)}, s32[]{:T(128)}, s32[2,4]{1,0:T(2,128)}, /*index=5*/f32[3,1024]{1,0:T(...) while((s32[]{:T(128)}, f32[3,1024]{1,0:T(4,128)S(1)}, ...), condition=%wide.region_11.12_spmd, body=%wide.region_5.11_spmd.sunk | while | flops 1671938432 | bytes 27035328 | solution.py:177
  688.9 1.3 constant_dynamic-slice_fusion.24
  691.6 0.9 convert_bitcast_fusion.2
  692.5 0.1 fusion.139
  692.6 0.8 dynamic-slice_convert_fusion.2
  693.4 0.2 add_multiply_fusion.2
  693.6 5.3 fusion.140
  699.0 9.3 fusion.142
  708.3 9.3 fusion.141
  717.6 0.3 subtract_divide_fusion.2
  717.9 0.2 fusion.143
  718.9 1.3 constant_dynamic-slice_fusion.24
  721.6 0.9 convert_bitcast_fusion.2
  722.5 0.8 dynamic-slice_convert_fusion.2
  723.3 0.2 add_multiply_fusion.2
  723.6 5.4 fusion.140
  728.9 9.3 fusion.142
  738.2 9.3 fusion.141
  747.6 0.3 subtract_divide_fusion.2
  747.9 0.2 fusion.143
  748.8 1.0 copy.55
  749.9 0.4 fusion.92
  750.3 2.0 copy.57
  752.4 0.7 copy.49
  753.1 125.7 %reduce-scatter.7.cloned.1.call-done = f32[128,3]{1,0:T(8,128)} async-done(((f32[1024,3]{1,0:T(8,128)}), f32[128,3]{1,0:T(8,128)}) %reduce-scatter.7.cloned.1.call-update) | async-done | bytes 1552
  878.8 0.9 copy.56
  879.7 122.0 %reduce-scatter.9.cloned.1.call-done = f32[128,3]{1,0:T(8,128)} async-done(((f32[4096,3]{1,0:T(8,128)}), f32[128,3]{1,0:T(8,128)}) %reduce-scatter.9.cloned.1.call-update) | async-done | bytes 1552
  1001.6 0.9 copy.58
  1002.5 0.6 add.299
  (60 shorter events, 1.1 us)
Async XLA Ops:
  7.2 680.1 %copy-start = (bf16[128,128]{1,0:T(8,128)(2,1)S(1)}, bf16[128,128]{1,0:T(8,128)(2,1)}, u32[]{:S(2)}) copy-start(bf16[128,128]{1,0:T(8,128)(2,1)} %param.29) | copy-start | bytes 98308
  7.2 621.7 %all-gather.2.cloned.1.call-start = ((), (), s32[]{:S(2)}) async-start(), calls=%async_computation.2 | async-start | bytes 1081344 | tf_op jit(solution)/shard_map/all_gather | solution.py:118
  8.8 870.0 %reduce-scatter.7.cloned.1.call-start = ((), (), s32[]{:S(2)}) async-start(), calls=%async_computation.3 | async-start | bytes 589824
  629.0 58.2 %copy-start.5 = (f32[128]{0:T(128)S(1)}, f32[128]{0:T(128)}, u32[]{:S(2)}) copy-start(f32[128]{0:T(128)} %param.30) | copy-start | bytes 1540
  688.0 61.9 %copy-start.3 = (bf16[128,128]{1,0:T(8,128)(2,1)S(1)}, bf16[128,128]{1,0:T(8,128)(2,1)}, u32[]{:S(2)}) copy-start(bf16[128,128]{1,0:T(8,128)(2,1)} %param.31) | copy-start | bytes 98308
  688.0 64.3 %copy-start.2 = (bf16[128,128]{0,1:T(8,128)(2,1)S(1)}, bf16[128,128]{0,1:T(8,128)(2,1)}, u32[]{:S(2)}) copy-start(bf16[128,128]{0,1:T(8,128)(2,1)} %copy.45) | copy-start | bytes 98308
  688.0 64.3 %copy-start.4 = (f32[128]{0:T(128)S(1)}, f32[128]{0:T(128)}, u32[]{:S(2)}) copy-start(f32[128]{0:T(128)} %param.32) | copy-start | bytes 1540
  688.9 10.1 copy-start.1
  688.9 10.1 copy-start.6
  699.0 9.3 copy-start.7
  718.8 10.1 copy-start.1
  718.8 10.1 copy-start.6
  728.9 9.3 copy-start.7
  749.8 251.8 %reduce-scatter.9.cloned.1.call-start = ((), (), s32[]{:S(2)}) async-start(), calls=%async_computation.4 | async-start | bytes 2162688
Sparse Core Ops, SparseCore 0:
  11.1 76.3 all-gather.1
  749.9 128.8 reduce-scatter.6
  883.5 118.0 reduce-scatter.8
where the time goes:
time: 1020 us; the launch traced here: 1010 us
  blocking collectives  646 us (63%)
  waiting for transfers between devices  248 us (24%)
  matrix products  68.5 us (7%)
  local copies, waits for them, and re-layouts  15.5 us (2%)
  between operations  13.9 us (1%)
    all_gather x1, blocking collectives, local(): lax.all_gather(positions, ('row', 'col'), axis=1, tiled=True)  617 us
    unnamed x5, waiting for transfers between devices  248 us
    dot_general x4, matrix products, filter_forward(): jnp.einsum('hf,hrc->frc', w_f2, hidden, preferred_element_type=jnp.float32)  35.6 us
    psum x1, blocking collectives, local(): block_messages_sum = lax.psum(partial_messages, 'col')  29.3 us
  transfers between devices with their start and end apart: 3, of which 2 were waited for; matrix products, arithmetic and copies ran while one was open for 1% of the time, Pallas kernels for 0%

commit v1 on v0

v1 whole, which is shorter than its diff:
```python
import functools
import math

import jax
import jax.numpy as jnp
from jax import lax
from jax.experimental import pallas as pl
from jax.experimental.pallas import tpu as pltpu
from jax.sharding import PartitionSpec as P

SOFTENING = 0.25
GAMMA_RBF = 10.0
CENTER_MAX = 10.0
CUTOFF = 12.0
LN2 = math.log(2.0)
SCALE = math.sqrt(GAMMA_RBF / LN2)
F32 = jnp.float32
BF16 = jnp.bfloat16
MESH = pl.DeviceIdType.MESH


def cos_sin(x):
    y = x * x
    cos_acc = jnp.full_like(y, 1.0 / math.factorial(14)) * -1.0
    for n in (12, 10, 8, 6, 4, 2, 0):
        sign = 1.0 if (n // 2) % 2 == 0 else -1.0
        cos_acc = cos_acc * y + sign / math.factorial(n)
    sin_acc = jnp.full_like(y, 1.0 / math.factorial(13))
    for n in (11, 9, 7, 5, 3, 1):
        sign = 1.0 if ((n - 1) // 2) % 2 == 0 else -1.0
        sin_acc = sin_acc * y + sign / math.factorial(n)
    return cos_acc, sin_acc * x


def pieces(value):
    high = value.astype(BF16)
    rest = value - high.astype(F32)
    mid = rest.astype(BF16)
    low = (rest - mid.astype(F32)).astype(BF16)
    return high, mid, low


def row16(row):
    block = jnp.broadcast_to(row, (16, row.shape[1])).astype(BF16)
    return jnp.concatenate([block] * 8, axis=0)


def kernel(
    n_row, n_col, n_slot,
    pairs_ref, count_ref, feat_ref, pos_ref, mask_ref,
    w_in_ref, w1_ref, b1_ref, w2_ref, b2_ref, wo1_ref, bo1_ref, wo2_ref, bo2_ref, rw_ref,
    fout_ref, force_ref,
    pos_row, pos_col, proj_own, proj_all,
    w1a, w2f, diag,
    dist, cm, cpm, unit,
    hid, msg, part, msg_in, grad_own, grad_all, grad_f, dgrad,
    rforce, cforce, rpart, cpart, rforce_in, cforce_in,
    prs, prr, pcs, pcr, js, jr, ms, mr, gs, gr, rfs, rfr, cfs, cfr,
):
    my_row = lax.axis_index("row")
    my_col = lax.axis_index("col")
    half = 64

    def row_peer(k):
        return lax.rem(my_row + k, n_row)

    def col_peer(k):
        return lax.rem(my_col + k, n_col)

    def to_row(src, dst, ssem, rsem, peer):
        return pltpu.make_async_remote_copy(
            src_ref=src, dst_ref=dst, send_sem=ssem, recv_sem=rsem,
            device_id={"row": peer}, device_id_type=MESH,
        )

    def to_col(src, dst, ssem, rsem, peer):
        return pltpu.make_async_remote_copy(
            src_ref=src, dst_ref=dst, send_sem=ssem, recv_sem=rsem,
            device_id={"col": peer}, device_id_type=MESH,
        )

    def each(n, body):
        def step(k, carry):
            body(k)
            return carry
        lax.fori_loop(1, n, step, 0)

    barrier = pltpu.get_barrier_semaphore()
    each(n_row, lambda k: pl.semaphore_signal(
        barrier, inc=1, device_id={"row": row_peer(k)}, device_id_type=MESH))
    each(n_col, lambda k: pl.semaphore_signal(
        barrier, inc=1, device_id={"col": col_peer(k)}, device_id_type=MESH))

    feat_t = jnp.transpose(feat_ref[...].astype(F32))
    proj_own[...] = jnp.dot(
        feat_t.astype(BF16), w_in_ref[...], preferred_element_type=F32
    ).astype(BF16)
    proj_all[my_row] = proj_own[...]
    pos_row[my_col] = pos_ref[...]
    pos_col[my_row] = pos_ref[...]

    bias = jnp.transpose(jnp.broadcast_to(b1_ref[...] - LN2, (128, 128)))
    high, mid, low = pieces(bias)
    lane = lax.broadcasted_iota(jnp.int32, (128, 128), 1)
    zero = jnp.zeros((128, 128), F32)
    extra = jnp.where(lane == 64, high.astype(F32), zero)
    extra = jnp.where(lane == 65, mid.astype(F32), extra)
    extra = jnp.where(lane == 66, low.astype(F32), extra)
    w1t = jnp.transpose(
        jnp.concatenate([w1_ref[...].astype(F32), jnp.zeros((64, 128), F32)], axis=0)
    )
    w1a[...] = (w1t + extra).astype(BF16)
    w2f[...] = w2_ref[...].astype(F32)
    diag[...] = jnp.zeros_like(diag)

    pl.semaphore_wait(barrier, n_row - 1 + n_col - 1)

    def pos_row_copy(k, src_index):
        return to_col(pos_ref, pos_row.at[src_index], pcs.at[k], pcr.at[src_index], col_peer(k))

    def pos_col_copy(k, src_index):
        return to_row(pos_ref, pos_col.at[src_index], prs.at[k], prr.at[src_index], row_peer(k))

    def proj_copy(k, src_index):
        return to_row(proj_own, proj_all.at[src_index], js.at[k], jr.at[src_index], row_peer(k))

    each(n_row, lambda k: pos_col_copy(k, my_row).start())
    each(n_col, lambda k: pos_row_copy(k, my_col).start())
    each(n_row, lambda k: proj_copy(k, my_row).start())
    each(n_row, lambda k: pos_col_copy(k, row_peer(k)).wait_recv())
    each(n_col, lambda k: pos_row_copy(k, col_peer(k)).wait_recv())

    def tiles_of(s):
        t = jnp.clip(pairs_ref[0, s], 0, n_col - 1)
        c = jnp.clip(pairs_ref[1, s], 0, n_row - 1)
        return t, c

    def geometry(s, carry):
        t, c = tiles_of(s)
        pr = pos_row[t]
        pc = pos_col[c]
        seps = []
        d2 = None
        for a in range(3):
            column = jnp.transpose(jnp.broadcast_to(pr[a:a + 1, :], (128, 128)))
            sep = column - pc[a:a + 1, :]
            seps.append(sep)
            d2 = sep * sep if d2 is None else d2 + sep * sep
        d2 = d2 + SOFTENING
        d = jnp.sqrt(d2)
        inv = 1.0 / d
        cos_h, sin_h = cos_sin(d * (0.5 * math.pi / CUTOFF))
        listed = jnp.where(s < count_ref[0, 0], 1.0, 0.0)
        m = mask_ref[s].astype(F32) * listed
        dist[s] = d * SCALE
        cm[s] = m * (cos_h * cos_h)
        cpm[s] = m * ((-math.pi / CUTOFF) * (sin_h * cos_h))
        for a in range(3):
            unit[s, a] = seps[a] * inv
        return carry

    lax.fori_loop(0, n_slot, geometry, 0)

    mu = lax.broadcasted_iota(jnp.int32, (64, 128), 0).astype(F32) * (
        CENTER_MAX / 63.0 * SCALE
    )
    ones = jnp.ones((16, 256), BF16)

    def rows_of(ref, s, ip):
        return ref[s, pl.ds(ip, 1), :], ref[s, pl.ds(ip + half, 1), :]

    def set_diag(c):
        p = proj_all[c]
        diag[0:128, 0:128] = p
        diag[128:256, 128:256] = p

    each(n_row, lambda k: proj_copy(k, row_peer(k)).wait_recv())

    def forward_slot(s, carry):
        t, c = tiles_of(s)
        set_diag(c)

        def step(ip, inner):
            d1, d2 = rows_of(dist, s, ip)
            x1 = d1 - mu
            x2 = d2 - mu
            g = jnp.concatenate(
                [jnp.exp2(-(x1 * x1)).astype(BF16), jnp.exp2(-(x2 * x2)).astype(BF16)], axis=1
            )
            rhs = jnp.concatenate([g, ones], axis=0)
            pre = jnp.dot(w1a[:, 0:80], rhs, preferred_element_type=F32)
            hidden = jnp.log(jnp.exp(pre) + 0.5).astype(BF16)
            hid[s, ip] = hidden
            c1, c2 = rows_of(cm, s, ip)
            scaled = hidden * row16(jnp.concatenate([c1, c2], axis=1))
            a = jnp.dot(scaled, diag[...], preferred_element_type=F32)
            w2 = w2f[...]
            msg[s, pl.ds(ip, 1), :] = jnp.sum(a[:, 0:128] * w2, axis=0, keepdims=True)
            msg[s, pl.ds(ip + half, 1), :] = jnp.sum(a[:, 128:256] * w2, axis=0, keepdims=True)
            return inner

        lax.fori_loop(0, half, step, 0)
        weight_sum = jnp.dot(
            cm[s].astype(BF16), diag[0:128, 0:128], preferred_element_type=F32
        )
        msg[s] = msg[s] + weight_sum * b2_ref[...]
        return carry

    lax.fori_loop(0, n_slot, forward_slot, 0)

    def gather_tile(tile, carry):
        total = None
        for s in range(n_slot):
            t, _ = tiles_of(s)
            term = msg[s] * jnp.where(t == tile, 1.0, 0.0)
            total = term if total is None else total + term
        part[tile] = total.astype(BF16)
        return carry

    lax.fori_loop(0, n_col, gather_tile, 0)
    msg_in[my_col] = part[my_col]

    def msg_copy(k, tile, src_index):
        return to_col(part.at[tile], msg_in.at[src_index], ms.at[k], mr.at[src_index], col_peer(k))

    each(n_col, lambda k: msg_copy(k, col_peer(k), my_col).start())

    def derivative_slot(s, carry):
        def step(ip, inner):
            d1, d2 = rows_of(dist, s, ip)
            x1 = d1 - mu
            x2 = d2 - mu
            factor = -2.0 * GAMMA_RBF / SCALE
            g1 = jnp.exp2(-(x1 * x1)) * (x1 * factor)
            g2 = jnp.exp2(-(x2 * x2)) * (x2 * factor)
            g = jnp.concatenate([g1.astype(BF16), g2.astype(BF16)], axis=1)
            slope = jnp.dot(w1a[:, 0:64], g, preferred_element_type=F32)
            hidden = hid[s, ip].astype(F32)
            sig = 1.0 - 0.5 * jnp.exp(-hidden)
            c1, c2 = rows_of(cm, s, ip)
            e1, e2 = rows_of(cpm, s, ip)
            c_row = jnp.concatenate([c1, c2], axis=1)
            e_row = jnp.concatenate([e1, e2], axis=1)
            hid[s, ip] = (slope * (sig * c_row) + hidden * e_row).astype(BF16)
            return inner

        lax.fori_loop(0, half, step, 0)
        return carry

    lax.fori_loop(0, n_slot, derivative_slot, 0)

    each(n_col, lambda k: msg_copy(k, col_peer(k), col_peer(k)).wait_recv())
    total = msg_in[0].astype(F32)
    for k in range(1, n_col):
        total = total + msg_in[k].astype(F32)
    pre = jnp.dot(total.astype(BF16), wo1_ref[...], preferred_element_type=F32) + bo1_ref[...]
    small = jnp.exp(-jnp.abs(pre))
    activated = (jnp.maximum(pre, 0.0) + jnp.log(1.0 + small) - LN2).astype(BF16)
    sig = jnp.where(pre >= 0.0, 1.0, small) / (1.0 + small)
    direction = lax.dot_general(
        jnp.broadcast_to(rw_ref[...], (8, 128)), wo2_ref[...].astype(F32),
        (((1,), (1,)), ((), ())), precision=lax.Precision.HIGHEST,
        preferred_element_type=F32,
    )[0:1, :]
    grad_own[...] = lax.dot_general(
        sig * direction, wo1_ref[...].astype(F32), (((1,), (1,)), ((), ())),
        precision=lax.Precision.HIGHEST, preferred_element_type=F32,
    ).astype(BF16)
    grad_all[my_col] = grad_own[...]

    def grad_copy(k, src_index):
        return to_col(grad_own, grad_all.at[src_index], gs.at[k], gr.at[src_index], col_peer(k))

    each(n_col, lambda k: grad_copy(k, my_col).start())
    update = jnp.dot(activated, wo2_ref[...], preferred_element_type=F32) + bo2_ref[...]
    fout_ref[...] = (feat_ref[...].astype(F32) + jnp.transpose(update)).astype(BF16)
    each(n_col, lambda k: grad_copy(k, col_peer(k)).wait_recv())

    def force_slot(s, carry):
        t, c = tiles_of(s)
        set_diag(c)
        grad_f[...] = grad_all[t].astype(F32)

        def step(ip, inner):
            r1 = grad_f[pl.ds(ip, 1), :]
            r2 = grad_f[pl.ds(ip + half, 1), :]
            w2 = w2_ref[...]
            lhs = jnp.concatenate([w2 * row16(r1), w2 * row16(r2)], axis=1)
            q = lax.dot_general(
                lhs, diag[...], (((1,), (1,)), ((), ())), preferred_element_type=F32
            )
            row = jnp.sum(q * hid[s, ip].astype(F32), axis=0, keepdims=True)
            dgrad[pl.ds(ip, 1), :] = row[:, 0:128]
            dgrad[pl.ds(ip + half, 1), :] = row[:, 128:256]
            return inner

        lax.fori_loop(0, half, step, 0)
        g_b2 = (grad_f[...] * b2_ref[...]).astype(BF16)
        plain = lax.dot_general(
            g_b2, diag[0:128, 0:128], (((1,), (1,)), ((), ())), preferred_element_type=F32
        )
        d = dgrad[...] + cpm[s] * plain
        rows, cols = [], []
        for a in range(3):
            push = unit[s, a] * d
            cols.append(jnp.sum(push, axis=0, keepdims=True))
            rows.append(-jnp.sum(jnp.transpose(push), axis=0, keepdims=True))
        pad = [jnp.zeros((5, 128), F32)]
        rforce[s] = jnp.concatenate(rows + pad, axis=0)
        cforce[s] = jnp.concatenate(cols + pad, axis=0)
        return carry

    lax.fori_loop(0, n_slot, force_slot, 0)

    def spread(source, target, which, n):
        def one(tile, carry):
            total = None
            for s in range(n_slot):
                term = source[s] * jnp.where(tiles_of(s)[which] == tile, 1.0, 0.0)
                total = term if total is None else total + term
            target[tile] = total
            return carry
        lax.fori_loop(0, n, one, 0)

    spread(cforce, cpart, 1, n_row)
    spread(rforce, rpart, 0, n_col)
    cforce_in[my_row] = cpart[my_row]
    rforce_in[my_col] = rpart[my_col]

    def cforce_copy(k, tile, src_index):
        return to_row(cpart.at[tile], cforce_in.at[src_index], cfs.at[k], cfr.at[src_index], row_peer(k))

    def rforce_copy(k, tile, src_index):
        return to_col(rpart.at[tile], rforce_in.at[src_index], rfs.at[k], rfr.at[src_index], col_peer(k))

    each(n_row, lambda k: cforce_copy(k, row_peer(k), my_row).start())
    each(n_col, lambda k: rforce_copy(k, col_peer(k), my_col).start())

    each(n_row, lambda k: pos_col_copy(k, my_row).wait_send())
    each(n_col, lambda k: pos_row_copy(k, my_col).wait_send())
    each(n_row, lambda k: proj_copy(k, my_row).wait_send())
    each(n_col, lambda k: msg_copy(k, col_peer(k), my_col).wait_send())
    each(n_col, lambda k: grad_copy(k, my_col).wait_send())

    each(n_col, lambda k: rforce_copy(k, col_peer(k), col_peer(k)).wait_recv())
    each(n_row, lambda k: cforce_copy(k, row_peer(k), row_peer(k)).wait_recv())
    force = rforce_in[0]
    for k in range(1, n_col):
        force = force + rforce_in[k]
    for k in range(n_row):
        force = force + cforce_in[k]
    force_ref[...] = force[0:3, :]
    each(n_row, lambda k: cforce_copy(k, row_peer(k), my_row).wait_send())
    each(n_col, lambda k: rforce_copy(k, col_peer(k), my_col).wait_send())


def solution(mesh):
    n_row, n_col = mesh.shape["row"], mesh.shape["col"]

    def local(features, positions, tile_pairs, pair_count, masks, w_in, w_f1, b_f1, w_f2, b_f2,
              w_o1, b_o1, w_o2, b_o2, read_w):
        n_slot = masks.shape[2]
        vmem = pl.BlockSpec(memory_space=pltpu.VMEM)
        smem = pl.BlockSpec(memory_space=pltpu.SMEM)
        tile = (128, 128)
        dma = pltpu.SemaphoreType.DMA
        return pl.pallas_call(
            functools.partial(kernel, n_row, n_col, n_slot),
            out_shape=(
                jax.ShapeDtypeStruct(features.shape, BF16),
                jax.ShapeDtypeStruct(positions.shape, F32),
            ),
            in_specs=[smem, smem] + [vmem] * 13,
            out_specs=(vmem, vmem),
            scratch_shapes=[
                pltpu.VMEM((n_col, 3, 128), F32),
                pltpu.VMEM((n_row, 3, 128), F32),
                pltpu.VMEM(tile, BF16),
                pltpu.VMEM((n_row,) + tile, BF16),
                pltpu.VMEM(tile, BF16),
                pltpu.VMEM(tile, F32),
                pltpu.VMEM((256, 256), BF16),
                pltpu.VMEM((n_slot,) + tile, F32),
                pltpu.VMEM((n_slot,) + tile, F32),
                pltpu.VMEM((n_slot,) + tile, F32),
                pltpu.VMEM((n_slot, 3) + tile, F32),
                pltpu.VMEM((n_slot, 64, 128, 256), BF16),
                pltpu.VMEM((n_slot,) + tile, F32),
                pltpu.VMEM((n_col,) + tile, BF16),
                pltpu.VMEM((n_col,) + tile, BF16),
                pltpu.VMEM(tile, BF16),
                pltpu.VMEM((n_col,) + tile, BF16),
                pltpu.VMEM(tile, F32),
                pltpu.VMEM(tile, F32),
                pltpu.VMEM((n_slot, 8, 128), F32),
                pltpu.VMEM((n_slot, 8, 128), F32),
                pltpu.VMEM((n_col, 8, 128), F32),
                pltpu.VMEM((n_row, 8, 128), F32),
                pltpu.VMEM((n_col, 8, 128), F32),
                pltpu.VMEM((n_row, 8, 128), F32),
                dma((n_row,)), dma((n_row,)),
                dma((n_col,)), dma((n_col,)),
                dma((n_row,)), dma((n_row,)),
                dma((n_col,)), dma((n_col,)),
                dma((n_col,)), dma((n_col,)),
                dma((n_col,)), dma((n_col,)),
                dma((n_row,)), dma((n_row,)),
            ],
            compiler_params=pltpu.CompilerParams(
                collective_id=0, has_side_effects=True, vmem_limit_bytes=56 << 20
            ),
        )(
            tile_pairs.reshape(tile_pairs.shape[2:]), pair_count, features, positions,
            masks.reshape(masks.shape[2:]),
            w_in, w_f1, b_f1.reshape(1, -1), w_f2, b_f2.reshape(1, -1),
            w_o1, b_o1.reshape(1, -1), w_o2, b_o2.reshape(1, -1), read_w.reshape(1, -1),
        )

    split = P(None, ("row", "col"))
    return jax.shard_map(
        local, mesh=mesh,
        in_specs=(split, split, P("row", "col", None, None), P("row", "col"),
                  P("row", "col", None, None, None)) + (P(),) * 10,
        out_specs=(split, split), check_vma=False,
    )
```

time: 1020 us -> 243 us (0.24)
  blocking collectives: 646 us -> 0 us
  waiting for transfers between devices: 248 us -> 0 us
  Pallas kernels: 0 us -> 240 us
  matrix products: 68.5 us -> 0 us
  local copies, waits for them, and re-layouts: 15.5 us -> 1.96 us
  between operations: 13.9 us -> 1.3 us
    all_gather x1 -> x0, blocking collectives: 617 us -> none  [local(): lax.all_gather(positions, ('row', 'col'), axis=1, tiled=True)]
    unnamed x5 -> x0, waiting for transfers between devices: 248 us -> none
    pallas_call x0 -> x1, Pallas kernels: none -> 240 us  [local(): pl.pallas_call(functools.partial(kernel, n_row, n_col, n_slot), out_shape...]
    dot_general x13 -> x0, matrix products: 68.5 us -> none  [the longest x4 35.6 us: filter_forward(): jnp.einsum('hf,hrc->frc', w_f2, hidden, preferred_element_type=jnp.float32)]
    psum x1 -> x0, blocking collectives: 29.3 us -> none  [local(): block_messages_sum = lax.psum(partial_messages, 'col')]
  transfers between devices with their start and end apart: 3 -> 0, of which waited for: 2 -> 0; matrix products, arithmetic and copies ran while one was open for 1% -> 0% of each run, Pallas kernels for 0% -> 0%
where the time goes in v1:
time: 243 us
  Pallas kernels  240 us (99%)
    pallas_call x1, Pallas kernels, local(): pl.pallas_call(functools.partial(kernel, n_row, n_col, n_slot), out_shape...  240 us

profile of v1, /device:TPU:1, one launch (start us, length us, event | category | flops | bytes accessed | tf_op | source)
XLA Modules:
  0.0 242.8 jit_solution(10374475683079244094)
XLA Ops:
  1.3 239.5 %shard_map.158 = (bf16[128,128]{1,0:T(8,128)(2,1)}, f32[3,128]{1,0:T(4,128)}) custom-call(s32[2,4]{1,0:T(2,128)} %bitcast.8, s32[1,1]{1,0:T(1,128)S(6)} %copy.19.count_ref, bf16[128,128]{1,0:T(8,128)(2,1)} %feat_ref.1, f32[3,128]{1,0:T(4,128)} %pos_ref.1, s32[4,128,128]{2,1,0:T(8,128)} %bitcast.7, bf16[128,128]{1,0:T(8,128)(2,1)} %w_in_ref.1, ...), custom_call_target="tpu_custom_call" | custom-call | tf_op jit(solution)/shard_map/pallas_call | solution.py:367
  240.8 0.0 copy-start
  240.8 1.4 copy.20
  242.2 0.0 copy-done
  242.2 0.6 copy.21
Async XLA Ops:
  240.8 1.4 copy-start

commit v2 on v1

--- a/solution.py
+++ b/solution.py
@@ -14,9 +14,14 @@
 CUTOFF = 12.0
 LN2 = math.log(2.0)
 SCALE = math.sqrt(GAMMA_RBF / LN2)
+SLOPE = -2.0 * GAMMA_RBF / SCALE
 F32 = jnp.float32
 BF16 = jnp.bfloat16
 MESH = pl.DeviceIdType.MESH
+PAIRS = 8
+HAND = 13
+LAG = 15
+SPLIT = 16
 
 
 def cos_sin(x):
@@ -50,12 +55,12 @@
     pairs_ref, count_ref, feat_ref, pos_ref, mask_ref,
     w_in_ref, w1_ref, b1_ref, w2_ref, b2_ref, wo1_ref, bo1_ref, wo2_ref, bo2_ref, rw_ref,
     fout_ref, force_ref,
-    pos_row, pos_col, proj_own, proj_all,
-    w1a, w2f, diag,
-    dist, cm, cpm, unit,
-    hid, msg, part, msg_in, grad_own, grad_all, grad_f, dgrad,
+    pos_row, pos_col, proj_all,
+    w1a, w1d, w2f, diag, diag_t,
+    dist, cm, cpm, ratio, unit,
+    hid, slope_in, msg, part, msg_in, grad_own, grad_all, grad_f, dgrad,
     rforce, cforce, rpart, cpart, rforce_in, cforce_in,
-    prs, prr, pcs, pcr, js, jr, ms, mr, gs, gr, rfs, rfr, cfs, cfr,
+    prs, prr, pcs, pcr, js, jh, jr, ms, mr, gs, gr, rfs, rfr, cfs, cfr,
 ):
     my_row = lax.axis_index("row")
     my_col = lax.axis_index("col")
@@ -91,11 +96,45 @@
     each(n_col, lambda k: pl.semaphore_signal(
         barrier, inc=1, device_id={"col": col_peer(k)}, device_id_type=MESH))
 
+    def pos_row_copy(k, src_index):
+        return to_col(pos_ref, pos_row.at[src_index], pcs.at[k], pcr.at[src_index], col_peer(k))
+
+    def pos_col_copy(k, src_index):
+        return to_row(pos_ref, pos_col.at[src_index], prs.at[k], prr.at[src_index], row_peer(k))
+
+    core = lax.rem(my_row, 2)
+    n_chip = n_row // 2
+
+    def chip_peer(k):
+        return lax.rem(my_row // 2 + k, n_chip) * 2 + core
+
+    def proj_copy(k, src_index):
+        return to_row(
+            proj_all.at[my_row], proj_all.at[src_index], js.at[k], jr.at[src_index], chip_peer(k)
+        )
+
+    def proj_hand(k):
+        return to_row(
+            proj_all.at[chip_peer(k)], proj_all.at[chip_peer(k)], jh.at[k], jr.at[chip_peer(k)],
+            my_row + 1 - 2 * core,
+        )
+
+    def proj_arrival(k):
+        src = chip_peer(k) + 1 - 2 * core
+        return to_row(
+            proj_all.at[src], proj_all.at[src], jh.at[k], jr.at[src], my_row + 1 - 2 * core
+        )
+
+    pl.semaphore_wait(barrier, n_row - 1 + n_col - 1)
+    each(n_row, lambda k: pos_col_copy(k, my_row).start())
+    each(n_col, lambda k: pos_row_copy(k, my_col).start())
+
     feat_t = jnp.transpose(feat_ref[...].astype(F32))
-    proj_own[...] = jnp.dot(
+    proj_all[my_row] = jnp.dot(
         feat_t.astype(BF16), w_in_ref[...], preferred_element_type=F32
     ).astype(BF16)
-    proj_all[my_row] = proj_own[...]
+    each(n_chip, lambda k: proj_copy(k, my_row).start())
+    proj_hand(0).start()
     pos_row[my_col] = pos_ref[...]
     pos_col[my_row] = pos_ref[...]
 
@@ -110,23 +149,9 @@
         jnp.concatenate([w1_ref[...].astype(F32), jnp.zeros((64, 128), F32)], axis=0)
     )
     w1a[...] = (w1t + extra).astype(BF16)
+    w1d[...] = w1t[:, 0:64].astype(BF16)
     w2f[...] = w2_ref[...].astype(F32)
-    diag[...] = jnp.zeros_like(diag)
-
-    pl.semaphore_wait(barrier, n_row - 1 + n_col - 1)
-
-    def pos_row_copy(k, src_index):
-        return to_col(pos_ref, pos_row.at[src_index], pcs.at[k], pcr.at[src_index], col_peer(k))
-
-    def pos_col_copy(k, src_index):
-        return to_row(pos_ref, pos_col.at[src_index], prs.at[k], prr.at[src_index], row_peer(k))
-
-    def proj_copy(k, src_index):
-        return to_row(proj_own, proj_all.at[src_index], js.at[k], jr.at[src_index], row_peer(k))
-
-    each(n_row, lambda k: pos_col_copy(k, my_row).start())
-    each(n_col, lambda k: pos_row_copy(k, my_col).start())
-    each(n_row, lambda k: proj_copy(k, my_row).start())
+
     each(n_row, lambda k: pos_col_copy(k, row_peer(k)).wait_recv())
     each(n_col, lambda k: pos_row_copy(k, col_peer(k)).wait_recv())
 
@@ -154,7 +179,9 @@
         m = mask_ref[s].astype(F32) * listed
         dist[s] = d * SCALE
         cm[s] = m * (cos_h * cos_h)
-        cpm[s] = m * ((-math.pi / CUTOFF) * (sin_h * cos_h))
+        slope_c = (-math.pi / CUTOFF) * sin_h
+        cpm[s] = m * (slope_c * cos_h)
+        ratio[s] = (LN2 / SLOPE) * (slope_c / cos_h)
         for a in range(3):
             unit[s, a] = seps[a] * inv
         return carry
@@ -165,48 +192,96 @@
         CENTER_MAX / 63.0 * SCALE
     )
     ones = jnp.ones((16, 256), BF16)
-
-    def rows_of(ref, s, ip):
-        return ref[s, pl.ds(ip, 1), :], ref[s, pl.ds(ip + half, 1), :]
-
-    def set_diag(c):
+    groups = half // PAIRS
+
+    def pair_row(ref, s, ip):
+        return jnp.concatenate(
+            [ref[s, pl.ds(ip, 1), :], ref[s, pl.ds(ip + half, 1), :]], axis=1
+        )
+
+    def hidden_group(n):
+        s, base = n // groups, lax.rem(n, groups) * PAIRS
+        for b in range(PAIRS):
+            ip = base + b
+            x = jnp.concatenate(
+                [dist[s, pl.ds(ip, 1), :] - mu, dist[s, pl.ds(ip + half, 1), :] - mu], axis=1
+            )
+            wide = jnp.exp2(-(x * x))
+            slope_in[s, ip] = (wide * x).astype(BF16)
+            g = wide.astype(BF16)
+            pre = jnp.dot(
+                w1a[:, 0:80], jnp.concatenate([g, ones], axis=0), preferred_element_type=F32
+            ).astype(BF16)
+            e = jnp.exp2(pre * jnp.asarray(1.0 / LN2, BF16))
+            hid[s, ip] = lax.log2(e + jnp.asarray(0.5, BF16))
+
+    def message_group(n):
+        s, base = n // groups, lax.rem(n, groups) * PAIRS
+        scaled = jnp.concatenate(
+            [hid[s, base + b] * row16(pair_row(cm, s, base + b) * LN2) for b in range(PAIRS)],
+            axis=0,
+        )
+        a = jnp.dot(scaled, diag[s], preferred_element_type=F32)
+        w2 = w2f[...]
+        for b in range(PAIRS):
+            part_a = a[b * 128:(b + 1) * 128]
+            msg[s, pl.ds(base + b, 1), :] = jnp.sum(part_a[:, 0:128] * w2, axis=0, keepdims=True)
+            msg[s, pl.ds(base + b + half, 1), :] = jnp.sum(
+                part_a[:, 128:256] * w2, axis=0, keepdims=True
+            )
+
+    total_groups = n_slot * groups
+
+    def run(first, last, body):
+        def step(n, carry):
+            body(n)
+            return carry
+        lax.fori_loop(first, last, step, 0)
+
+    run(0, HAND, hidden_group)
+
+    def hand_on(k):
+        proj_copy(k, chip_peer(k)).wait_recv()
+        proj_hand(k).start()
+
+    each(n_chip, hand_on)
+
+    run(HAND, LAG, hidden_group)
+    proj_arrival(0).wait_recv()
+    each(n_chip, lambda k: proj_arrival(k).wait_recv())
+
+    def set_diag(s, carry):
+        _, c = tiles_of(s)
         p = proj_all[c]
-        diag[0:128, 0:128] = p
-        diag[128:256, 128:256] = p
-
-    each(n_row, lambda k: proj_copy(k, row_peer(k)).wait_recv())
-
-    def forward_slot(s, carry):
-        t, c = tiles_of(s)
-        set_diag(c)
-
-        def step(ip, inner):
-            d1, d2 = rows_of(dist, s, ip)
-            x1 = d1 - mu
-            x2 = d2 - mu
-            g = jnp.concatenate(
-                [jnp.exp2(-(x1 * x1)).astype(BF16), jnp.exp2(-(x2 * x2)).astype(BF16)], axis=1
-            )
-            rhs = jnp.concatenate([g, ones], axis=0)
-            pre = jnp.dot(w1a[:, 0:80], rhs, preferred_element_type=F32)
-            hidden = jnp.log(jnp.exp(pre) + 0.5).astype(BF16)
-            hid[s, ip] = hidden
-            c1, c2 = rows_of(cm, s, ip)
-            scaled = hidden * row16(jnp.concatenate([c1, c2], axis=1))
-            a = jnp.dot(scaled, diag[...], preferred_element_type=F32)
-            w2 = w2f[...]
-            msg[s, pl.ds(ip, 1), :] = jnp.sum(a[:, 0:128] * w2, axis=0, keepdims=True)
-            msg[s, pl.ds(ip + half, 1), :] = jnp.sum(a[:, 128:256] * w2, axis=0, keepdims=True)
-            return inner
-
-        lax.fori_loop(0, half, step, 0)
+        z = jnp.zeros((128, 128), BF16)
+        diag[s, 0:128, 0:128] = p
+        diag[s, 0:128, 128:256] = z
+        diag[s, 128:256, 0:128] = z
+        diag[s, 128:256, 128:256] = p
+        q = jnp.transpose(p.astype(F32)).astype(BF16)
+        diag_t[s, 0:128, 0:128] = q
+        diag_t[s, 0:128, 128:256] = z
+        diag_t[s, 128:256, 0:128] = z
+        diag_t[s, 128:256, 128:256] = q
+        return carry
+
+    lax.fori_loop(0, n_slot, set_diag, 0)
+
+    def both(n):
+        message_group(n - LAG)
+        hidden_group(n)
+
+    run(LAG, total_groups, both)
+    run(total_groups - LAG, total_groups, message_group)
+
+    def add_bias(s, carry):
         weight_sum = jnp.dot(
-            cm[s].astype(BF16), diag[0:128, 0:128], preferred_element_type=F32
+            cm[s].astype(BF16), diag[s, 0:128, 0:128], preferred_element_type=F32
         )
         msg[s] = msg[s] + weight_sum * b2_ref[...]
         return carry
 
-    lax.fori_loop(0, n_slot, forward_slot, 0)
+    lax.fori_loop(0, n_slot, add_bias, 0)
 
     def gather_tile(tile, carry):
         total = None
@@ -225,29 +300,18 @@
 
     each(n_col, lambda k: msg_copy(k, col_peer(k), my_col).start())
 
-    def derivative_slot(s, carry):
-        def step(ip, inner):
-            d1, d2 = rows_of(dist, s, ip)
-            x1 = d1 - mu
-            x2 = d2 - mu
-            factor = -2.0 * GAMMA_RBF / SCALE
-            g1 = jnp.exp2(-(x1 * x1)) * (x1 * factor)
-            g2 = jnp.exp2(-(x2 * x2)) * (x2 * factor)
-            g = jnp.concatenate([g1.astype(BF16), g2.astype(BF16)], axis=1)
-            slope = jnp.dot(w1a[:, 0:64], g, preferred_element_type=F32)
-            hidden = hid[s, ip].astype(F32)
-            sig = 1.0 - 0.5 * jnp.exp(-hidden)
-            c1, c2 = rows_of(cm, s, ip)
-            e1, e2 = rows_of(cpm, s, ip)
-            c_row = jnp.concatenate([c1, c2], axis=1)
-            e_row = jnp.concatenate([e1, e2], axis=1)
-            hid[s, ip] = (slope * (sig * c_row) + hidden * e_row).astype(BF16)
-            return inner
-
-        lax.fori_loop(0, half, step, 0)
-        return carry
-
-    lax.fori_loop(0, n_slot, derivative_slot, 0)
+    def derivative_group(n):
+        s, base = n // groups, lax.rem(n, groups) * PAIRS
+        for b in range(PAIRS):
+            ip = base + b
+            slope = jnp.dot(
+                w1d[...], slope_in[s, ip], preferred_element_type=F32
+            ).astype(BF16)
+            level = hid[s, ip]
+            sig = jnp.asarray(1.0, BF16) - jnp.exp2(jnp.asarray(-1.0, BF16) - level)
+            hid[s, ip] = slope * sig + level * row16(pair_row(ratio, s, ip))
+
+    run(0, SPLIT, derivative_group)
 
     each(n_col, lambda k: msg_copy(k, col_peer(k), col_peer(k)).wait_recv())
     total = msg_in[0].astype(F32)
@@ -274,32 +338,46 @@
     each(n_col, lambda k: grad_copy(k, my_col).start())
     update = jnp.dot(activated, wo2_ref[...], preferred_element_type=F32) + bo2_ref[...]
     fout_ref[...] = (feat_ref[...].astype(F32) + jnp.transpose(update)).astype(BF16)
+    run(SPLIT, total_groups, derivative_group)
     each(n_col, lambda k: grad_copy(k, col_peer(k)).wait_recv())
 
+    def spread_grad(s, carry):
+        t, _ = tiles_of(s)
+        grad_f[s] = grad_all[t].astype(F32)
+        return carry
+
+    lax.fori_loop(0, n_slot, spread_grad, 0)
+
+    def dist_group(n):
+        s, base = n // groups, lax.rem(n, groups) * PAIRS
+        w2 = w2_ref[...]
+        lhs = jnp.concatenate(
+            [
+                jnp.concatenate(
+                    [
+                        w2 * row16(grad_f[s, pl.ds(base + b, 1), :]),
+                        w2 * row16(grad_f[s, pl.ds(base + b + half, 1), :]),
+                    ],
+                    axis=1,
+                )
+                for b in range(PAIRS)
+            ],
+            axis=0,
+        )
+        q = jnp.dot(lhs, diag_t[s], preferred_element_type=F32)
+        for b in range(PAIRS):
+            product = q[b * 128:(b + 1) * 128].astype(BF16) * hid[s, base + b]
+            folded = (product[0:64] + product[64:128]).astype(F32)
+            row = jnp.sum(folded, axis=0, keepdims=True)
+            dgrad[s, pl.ds(base + b, 1), :] = row[:, 0:128]
+            dgrad[s, pl.ds(base + b + half, 1), :] = row[:, 128:256]
+
+    run(0, total_groups, dist_group)
+
     def force_slot(s, carry):
-        t, c = tiles_of(s)
-        set_diag(c)
-        grad_f[...] = grad_all[t].astype(F32)
-
-        def step(ip, inner):
-            r1 = grad_f[pl.ds(ip, 1), :]
-            r2 = grad_f[pl.ds(ip + half, 1), :]
-            w2 = w2_ref[...]
-            lhs = jnp.concatenate([w2 * row16(r1), w2 * row16(r2)], axis=1)
-            q = lax.dot_general(
-                lhs, diag[...], (((1,), (1,)), ((), ())), preferred_element_type=F32
-            )
-            row = jnp.sum(q * hid[s, ip].astype(F32), axis=0, keepdims=True)
-            dgrad[pl.ds(ip, 1), :] = row[:, 0:128]
-            dgrad[pl.ds(ip + half, 1), :] = row[:, 128:256]
-            return inner
-
-        lax.fori_loop(0, half, step, 0)
-        g_b2 = (grad_f[...] * b2_ref[...]).astype(BF16)
-        plain = lax.dot_general(
-            g_b2, diag[0:128, 0:128], (((1,), (1,)), ((), ())), preferred_element_type=F32
-        )
-        d = dgrad[...] + cpm[s] * plain
+        g_b2 = (grad_f[s] * b2_ref[...]).astype(BF16)
+        plain = jnp.dot(g_b2, diag_t[s, 0:128, 0:128], preferred_element_type=F32)
+        d = dgrad[s] * (cm[s] * SLOPE) + cpm[s] * plain
         rows, cols = [], []
         for a in range(3):
             push = unit[s, a] * d
@@ -338,7 +416,9 @@
 
     each(n_row, lambda k: pos_col_copy(k, my_row).wait_send())
     each(n_col, lambda k: pos_row_copy(k, my_col).wait_send())
-    each(n_row, lambda k: proj_copy(k, my_row).wait_send())
+    each(n_chip, lambda k: proj_copy(k, my_row).wait_send())
+    proj_hand(0).wait_send()
+    each(n_chip, lambda k: proj_hand(k).wait_send())
     each(n_col, lambda k: msg_copy(k, col_peer(k), my_col).wait_send())
     each(n_col, lambda k: grad_copy(k, my_col).wait_send())
 
@@ -375,23 +455,26 @@
             scratch_shapes=[
                 pltpu.VMEM((n_col, 3, 128), F32),
                 pltpu.VMEM((n_row, 3, 128), F32),
-                pltpu.VMEM(tile, BF16),
                 pltpu.VMEM((n_row,) + tile, BF16),
                 pltpu.VMEM(tile, BF16),
+                pltpu.VMEM((128, 64), BF16),
                 pltpu.VMEM(tile, F32),
-                pltpu.VMEM((256, 256), BF16),
+                pltpu.VMEM((n_slot, 256, 256), BF16),
+                pltpu.VMEM((n_slot, 256, 256), BF16),
+                pltpu.VMEM((n_slot,) + tile, F32),
                 pltpu.VMEM((n_slot,) + tile, F32),
                 pltpu.VMEM((n_slot,) + tile, F32),
                 pltpu.VMEM((n_slot,) + tile, F32),
                 pltpu.VMEM((n_slot, 3) + tile, F32),
                 pltpu.VMEM((n_slot, 64, 128, 256), BF16),
+                pltpu.VMEM((n_slot, 64, 64, 256), BF16),
                 pltpu.VMEM((n_slot,) + tile, F32),
                 pltpu.VMEM((n_col,) + tile, BF16),
                 pltpu.VMEM((n_col,) + tile, BF16),
                 pltpu.VMEM(tile, BF16),
                 pltpu.VMEM((n_col,) + tile, BF16),
-                pltpu.VMEM(tile, F32),
-                pltpu.VMEM(tile, F32),
+                pltpu.VMEM((n_slot,) + tile, F32),
+                pltpu.VMEM((n_slot,) + tile, F32),
                 pltpu.VMEM((n_slot, 8, 128), F32),
                 pltpu.VMEM((n_slot, 8, 128), F32),
                 pltpu.VMEM((n_col, 8, 128), F32),
@@ -400,7 +483,7 @@
                 pltpu.VMEM((n_row, 8, 128), F32),
                 dma((n_row,)), dma((n_row,)),
                 dma((n_col,)), dma((n_col,)),
-                dma((n_row,)), dma((n_row,)),
+                dma((n_row // 2,)), dma((n_row // 2,)), dma((n_row,)),
                 dma((n_col,)), dma((n_col,)),
                 dma((n_col,)), dma((n_col,)),
                 dma((n_col,)), dma((n_col,)),

time: 243 us -> 83.4 us (0.34)
  Pallas kernels: 240 us -> 80 us
    pallas_call x1, Pallas kernels: 240 us -> 80 us  [local(): pl.pallas_call(functools.partial(kernel, n_row, n_col, n_slot), out_shape...]
where the time goes in v2:
time: 83.4 us; the launch traced here: 83.3 us
  Pallas kernels  80 us (96%)
  local copies, waits for them, and re-layouts  1.96 us (2%)
  between operations  1.3 us (2%)
    pallas_call x1, Pallas kernels, local(): pl.pallas_call(functools.partial(kernel, n_row, n_col, n_slot), out_shape...  80 us
    unnamed x4, local copies, waits for them, and re-layouts  1.96 us

profile of v2, /device:TPU:1, one launch (start us, length us, event | category | flops | bytes accessed | tf_op | source)
XLA Modules:
  0.0 83.3 jit_solution(3105271908035079071)
XLA Ops:
  1.3 80.0 %shard_map.158 = (bf16[128,128]{1,0:T(8,128)(2,1)}, f32[3,128]{1,0:T(4,128)}) custom-call(s32[2,4]{1,0:T(2,128)} %bitcast.8, s32[1,1]{1,0:T(1,128)S(6)} %copy.19.count_ref, bf16[128,128]{1,0:T(8,128)(2,1)} %feat_ref.1, f32[3,128]{1,0:T(4,128)} %pos_ref.1, s32[4,128,128]{2,1,0:T(8,128)} %bitcast.7, bf16[128,128]{1,0:T(8,128)(2,1)} %w_in_ref.1, ...), custom_call_target="tpu_custom_call" | custom-call | tf_op jit(solution)/shard_map/pallas_call | solution.py:447
  81.3 0.0 copy-start
  81.3 1.4 %copy.20 = bf16[128,128]{1,0:T(8,128)(2,1)} copy(bf16[128,128]{1,0:T(8,128)(2,1)} %get-tuple-element.4) | data formatting | bytes 65536
  82.7 0.0 copy-done
  82.7 0.6 copy.21
Async XLA Ops:
  81.3 1.4 %copy-start = (f32[3,128]{1,0:T(4,128)S(1)}, f32[3,128]{1,0:T(4,128)}, u32[]{:S(2)}) copy-start(f32[3,128]{1,0:T(4,128)} %get-tuple-element.5) | copy-start | bytes 4612

commit v3 on v2

--- a/solution.py
+++ b/solution.py
@@ -18,10 +18,10 @@
 F32 = jnp.float32
 BF16 = jnp.bfloat16
 MESH = pl.DeviceIdType.MESH
-PAIRS = 8
-HAND = 13
-LAG = 15
-SPLIT = 16
+PAIRS = 32
+HAND = 4
+LAG = 5
+SPLIT = 4
 
 
 def cos_sin(x):
@@ -396,7 +396,7 @@
             for s in range(n_slot):
                 term = source[s] * jnp.where(tiles_of(s)[which] == tile, 1.0, 0.0)
                 total = term if total is None else total + term
-            target[tile] = total
+            target[tile] = total[0:3]
             return carry
         lax.fori_loop(0, n, one, 0)
 
@@ -429,7 +429,7 @@
         force = force + rforce_in[k]
     for k in range(n_row):
         force = force + cforce_in[k]
-    force_ref[...] = force[0:3, :]
+    force_ref[...] = force
     each(n_row, lambda k: cforce_copy(k, row_peer(k), my_row).wait_send())
     each(n_col, lambda k: rforce_copy(k, col_peer(k), my_col).wait_send())
 
@@ -477,10 +477,10 @@
                 pltpu.VMEM((n_slot,) + tile, F32),
                 pltpu.VMEM((n_slot, 8, 128), F32),
                 pltpu.VMEM((n_slot, 8, 128), F32),
-                pltpu.VMEM((n_col, 8, 128), F32),
-                pltpu.VMEM((n_row, 8, 128), F32),
-                pltpu.VMEM((n_col, 8, 128), F32),
-                pltpu.VMEM((n_row, 8, 128), F32),
+                pltpu.VMEM((n_col, 3, 128), F32),
+                pltpu.VMEM((n_row, 3, 128), F32),
+                pltpu.VMEM((n_col, 3, 128), F32),
+                pltpu.VMEM((n_row, 3, 128), F32),
                 dma((n_row,)), dma((n_row,)),
                 dma((n_col,)), dma((n_col,)),
                 dma((n_row // 2,)), dma((n_row // 2,)), dma((n_row,)),

time: 83.4 us -> 72.9 us (0.87)
  Pallas kernels: 80 us -> 69.5 us
    pallas_call x1, Pallas kernels: 80 us -> 69.5 us  [local(): pl.pallas_call(functools.partial(kernel, n_row, n_col, n_slot), out_shape...]
where the time goes in v3:
time: 72.9 us; the launch traced here: 72.7 us
  Pallas kernels  69.5 us (95%)
  local copies, waits for them, and re-layouts  1.96 us (3%)
  between operations  1.3 us (2%)
    pallas_call x1, Pallas kernels, local(): pl.pallas_call(functools.partial(kernel, n_row, n_col, n_slot), out_shape...  69.5 us
    unnamed x4, local copies, waits for them, and re-layouts  1.96 us

profile of v3, /device:TPU:1, one launch (start us, length us, event | category | flops | bytes accessed | tf_op | source)
XLA Modules:
  0.0 72.7 jit_solution(7168018204347032503)
XLA Ops:
  1.3 69.5 %shard_map.158 = (bf16[128,128]{1,0:T(8,128)(2,1)}, f32[3,128]{1,0:T(4,128)}) custom-call(s32[2,4]{1,0:T(2,128)} %bitcast.8, s32[1,1]{1,0:T(1,128)S(6)} %copy.19.count_ref, bf16[128,128]{1,0:T(8,128)(2,1)} %feat_ref.1, f32[3,128]{1,0:T(4,128)} %pos_ref.1, s32[4,128,128]{2,1,0:T(8,128)} %bitcast.7, bf16[128,128]{1,0:T(8,128)(2,1)} %w_in_ref.1, ...), custom_call_target="tpu_custom_call" | custom-call | tf_op jit(solution)/shard_map/pallas_call | solution.py:447
  70.8 0.0 copy-start
  70.8 1.4 %copy.20 = bf16[128,128]{1,0:T(8,128)(2,1)} copy(bf16[128,128]{1,0:T(8,128)(2,1)} %get-tuple-element.4) | data formatting | bytes 65536
  72.1 0.0 copy-done
  72.1 0.6 copy.21
Async XLA Ops:
  70.8 1.4 %copy-start = (f32[3,128]{1,0:T(4,128)S(1)}, f32[3,128]{1,0:T(4,128)}, u32[]{:S(2)}) copy-start(f32[3,128]{1,0:T(4,128)} %get-tuple-element.5) | copy-start | bytes 4612

commit v4 on v3

--- a/solution.py
+++ b/solution.py
@@ -19,9 +19,10 @@
 BF16 = jnp.bfloat16
 MESH = pl.DeviceIdType.MESH
 PAIRS = 32
+PASS = 0
 HAND = 4
 LAG = 5
-SPLIT = 4
+SPLITS = (2, 5)
 
 
 def cos_sin(x):
@@ -58,13 +59,14 @@
     pos_row, pos_col, proj_all,
     w1a, w1d, w2f, diag, diag_t,
     dist, cm, cpm, ratio, unit,
-    hid, slope_in, msg, part, msg_in, grad_own, grad_all, grad_f, dgrad,
+    hid, slope_in, msg, part, msg_in, grad_own, grad_a, grad_b, update, grad_f, dgrad,
     rforce, cforce, rpart, cpart, rforce_in, cforce_in,
-    prs, prr, pcs, pcr, js, jh, jr, ms, mr, gs, gr, rfs, rfr, cfs, cfr,
+    prs, prr, pcs, pcr, js, jt, jh, jr, ms, mr, gs, gr, rfs, rfr, cfs, cfr,
 ):
     my_row = lax.axis_index("row")
     my_col = lax.axis_index("col")
     half = 64
+    grad_all = (grad_a, grad_b)
 
     def row_peer(k):
         return lax.rem(my_row + k, n_row)
@@ -103,27 +105,43 @@
         return to_row(pos_ref, pos_col.at[src_index], prs.at[k], prr.at[src_index], row_peer(k))
 
     core = lax.rem(my_row, 2)
-    n_chip = n_row // 2
-
-    def chip_peer(k):
-        return lax.rem(my_row // 2 + k, n_chip) * 2 + core
-
-    def proj_copy(k, src_index):
-        return to_row(
-            proj_all.at[my_row], proj_all.at[src_index], js.at[k], jr.at[src_index], chip_peer(k)
-        )
-
-    def proj_hand(k):
-        return to_row(
-            proj_all.at[chip_peer(k)], proj_all.at[chip_peer(k)], jh.at[k], jr.at[chip_peer(k)],
-            my_row + 1 - 2 * core,
-        )
-
-    def proj_arrival(k):
-        src = chip_peer(k) + 1 - 2 * core
-        return to_row(
-            proj_all.at[src], proj_all.at[src], jh.at[k], jr.at[src], my_row + 1 - 2 * core
-        )
+    n_ring = n_row // 4
+    ring = my_row // (2 * n_ring)
+    spot = lax.rem(my_row // 2, n_ring)
+
+    def on_ring(which, k):
+        return (which * n_ring + lax.rem(spot + k, n_ring)) * 2 + core
+
+    def other_core(row):
+        return row + 1 - 2 * core
+
+    def near(k):
+        return on_ring(ring, k)
+
+    def far(k):
+        return on_ring(1 - ring, k)
+
+    def tile_copy(tile, sem, peer):
+        return to_row(proj_all.at[tile], proj_all.at[tile], sem, jr.at[tile], peer)
+
+    def ring_copy(k):
+        return tile_copy(my_row, js.at[k], near(k))
+
+    def twin_copy(k):
+        return tile_copy(near(k), jt.at[k], far(0))
+
+    def hand_near(k):
+        return tile_copy(near(k), jh.at[k], other_core(my_row))
+
+    def hand_far(k):
+        return tile_copy(far(k), jh.at[n_ring + k], other_core(my_row))
+
+    def arrival(tile):
+        tile_copy(tile, js.at[0], other_core(my_row)).wait_recv()
+
+    def every(n, body):
+        body(0)
+        each(n, body)
 
     pl.semaphore_wait(barrier, n_row - 1 + n_col - 1)
     each(n_row, lambda k: pos_col_copy(k, my_row).start())
@@ -133,8 +151,9 @@
     proj_all[my_row] = jnp.dot(
         feat_t.astype(BF16), w_in_ref[...], preferred_element_type=F32
     ).astype(BF16)
-    each(n_chip, lambda k: proj_copy(k, my_row).start())
-    proj_hand(0).start()
+    each(n_ring, lambda k: ring_copy(k).start())
+    twin_copy(0).start()
+    hand_near(0).start()
     pos_row[my_col] = pos_ref[...]
     pos_col[my_row] = pos_ref[...]
 
@@ -194,17 +213,24 @@
     ones = jnp.ones((16, 256), BF16)
     groups = half // PAIRS
 
-    def pair_row(ref, s, ip):
+    def place(n):
+        return lax.rem(n, n_slot), n // n_slot * PAIRS
+
+    def pair_row(ref, s, row):
         return jnp.concatenate(
-            [ref[s, pl.ds(ip, 1), :], ref[s, pl.ds(ip + half, 1), :]], axis=1
+            [ref[s, pl.ds(row, 1), :], ref[s, pl.ds(row + PAIRS, 1), :]], axis=1
         )
 
     def hidden_group(n):
-        s, base = n // groups, lax.rem(n, groups) * PAIRS
+        s, base = place(n)
         for b in range(PAIRS):
             ip = base + b
             x = jnp.concatenate(
-                [dist[s, pl.ds(ip, 1), :] - mu, dist[s, pl.ds(ip + half, 1), :] - mu], axis=1
+                [
+                    dist[s, pl.ds(2 * base + b, 1), :] - mu,
+                    dist[s, pl.ds(2 * base + b + PAIRS, 1), :] - mu,
+                ],
+                axis=1,
             )
             wide = jnp.exp2(-(x * x))
             slope_in[s, ip] = (wide * x).astype(BF16)
@@ -216,17 +242,17 @@
             hid[s, ip] = lax.log2(e + jnp.asarray(0.5, BF16))
 
     def message_group(n):
-        s, base = n // groups, lax.rem(n, groups) * PAIRS
+        s, base = place(n)
         scaled = jnp.concatenate(
-            [hid[s, base + b] * row16(pair_row(cm, s, base + b) * LN2) for b in range(PAIRS)],
+            [hid[s, base + b] * row16(pair_row(cm, s, 2 * base + b) * LN2) for b in range(PAIRS)],
             axis=0,
         )
         a = jnp.dot(scaled, diag[s], preferred_element_type=F32)
         w2 = w2f[...]
         for b in range(PAIRS):
             part_a = a[b * 128:(b + 1) * 128]
-            msg[s, pl.ds(base + b, 1), :] = jnp.sum(part_a[:, 0:128] * w2, axis=0, keepdims=True)
-            msg[s, pl.ds(base + b + half, 1), :] = jnp.sum(
+            msg[s, pl.ds(2 * base + b, 1), :] = jnp.sum(part_a[:, 0:128] * w2, axis=0, keepdims=True)
+            msg[s, pl.ds(2 * base + b + PAIRS, 1), :] = jnp.sum(
                 part_a[:, 128:256] * w2, axis=0, keepdims=True
             )
 
@@ -238,17 +264,25 @@
             return carry
         lax.fori_loop(first, last, step, 0)
 
-    run(0, HAND, hidden_group)
-
-    def hand_on(k):
-        proj_copy(k, chip_peer(k)).wait_recv()
-        proj_hand(k).start()
-
-    each(n_chip, hand_on)
-
+    def pass_near(k):
+        arrival(near(k))
+        twin_copy(k).start()
+        hand_near(k).start()
+
+    def pass_far(k):
+        arrival(far(k))
+        hand_far(k).start()
+
+    def arrive_pair(k):
+        arrival(other_core(near(k)))
+        arrival(other_core(far(k)))
+
+    run(0, PASS, hidden_group)
+    each(n_ring, pass_near)
+    run(PASS, HAND, hidden_group)
+    every(n_ring, pass_far)
     run(HAND, LAG, hidden_group)
-    proj_arrival(0).wait_recv()
-    each(n_chip, lambda k: proj_arrival(k).wait_recv())
+    every(n_ring, arrive_pair)
 
     def set_diag(s, carry):
         _, c = tiles_of(s)
@@ -272,36 +306,48 @@
         hidden_group(n)
 
     run(LAG, total_groups, both)
-    run(total_groups - LAG, total_groups, message_group)
-
-    def add_bias(s, carry):
-        weight_sum = jnp.dot(
-            cm[s].astype(BF16), diag[s, 0:128, 0:128], preferred_element_type=F32
-        )
-        msg[s] = msg[s] + weight_sum * b2_ref[...]
-        return carry
-
-    lax.fori_loop(0, n_slot, add_bias, 0)
-
-    def gather_tile(tile, carry):
-        total = None
-        for s in range(n_slot):
-            t, _ = tiles_of(s)
-            term = msg[s] * jnp.where(t == tile, 1.0, 0.0)
-            total = term if total is None else total + term
-        part[tile] = total.astype(BF16)
-        return carry
-
-    lax.fori_loop(0, n_col, gather_tile, 0)
-    msg_in[my_col] = part[my_col]
-
-    def msg_copy(k, tile, src_index):
-        return to_col(part.at[tile], msg_in.at[src_index], ms.at[k], mr.at[src_index], col_peer(k))
-
-    each(n_col, lambda k: msg_copy(k, col_peer(k), my_col).start())
+
+    span = 2 * PAIRS
+
+    def part_rows(h):
+        return slice(h * span, (h + 1) * span)
+
+    def add_bias(h):
+        def body(s, carry):
+            weight_sum = jnp.dot(
+                cm[s, part_rows(h)].astype(BF16), diag[s, 0:128, 0:128],
+                preferred_element_type=F32,
+            )
+            msg[s, part_rows(h)] = msg[s, part_rows(h)] + weight_sum * b2_ref[...]
+            return carry
+        lax.fori_loop(0, n_slot, body, 0)
+
+    def gather_part(h):
+        def body(tile, carry):
+            total = None
+            for s in range(n_slot):
+                t, _ = tiles_of(s)
+                term = msg[s, part_rows(h)] * jnp.where(t == tile, 1.0, 0.0)
+                total = term if total is None else total + term
+            part[h, tile] = total.astype(BF16)
+            return carry
+        lax.fori_loop(0, n_col, body, 0)
+        msg_in[h, my_col] = part[h, my_col]
+
+    def msg_copy(h, k, tile, src_index):
+        return to_col(
+            part.at[h, tile], msg_in.at[h, src_index], ms.at[h * n_col + k],
+            mr.at[h * n_col + src_index], col_peer(k),
+        )
+
+    for h in range(groups):
+        run(max(total_groups - LAG, h * n_slot), (h + 1) * n_slot, message_group)
+        add_bias(h)
+        gather_part(h)
+        each(n_col, lambda k, h=h: msg_copy(h, k, col_peer(k), my_col).start())
 
     def derivative_group(n):
-        s, base = n // groups, lax.rem(n, groups) * PAIRS
+        s, base = place(n)
         for b in range(PAIRS):
             ip = base + b
             slope = jnp.dot(
@@ -309,54 +355,63 @@
             ).astype(BF16)
             level = hid[s, ip]
             sig = jnp.asarray(1.0, BF16) - jnp.exp2(jnp.asarray(-1.0, BF16) - level)
-            hid[s, ip] = slope * sig + level * row16(pair_row(ratio, s, ip))
-
-    run(0, SPLIT, derivative_group)
-
-    each(n_col, lambda k: msg_copy(k, col_peer(k), col_peer(k)).wait_recv())
-    total = msg_in[0].astype(F32)
-    for k in range(1, n_col):
-        total = total + msg_in[k].astype(F32)
-    pre = jnp.dot(total.astype(BF16), wo1_ref[...], preferred_element_type=F32) + bo1_ref[...]
-    small = jnp.exp(-jnp.abs(pre))
-    activated = (jnp.maximum(pre, 0.0) + jnp.log(1.0 + small) - LN2).astype(BF16)
-    sig = jnp.where(pre >= 0.0, 1.0, small) / (1.0 + small)
+            hid[s, ip] = slope * sig + level * row16(pair_row(ratio, s, 2 * base + b))
+
     direction = lax.dot_general(
         jnp.broadcast_to(rw_ref[...], (8, 128)), wo2_ref[...].astype(F32),
         (((1,), (1,)), ((), ())), precision=lax.Precision.HIGHEST,
         preferred_element_type=F32,
     )[0:1, :]
-    grad_own[...] = lax.dot_general(
-        sig * direction, wo1_ref[...].astype(F32), (((1,), (1,)), ((), ())),
-        precision=lax.Precision.HIGHEST, preferred_element_type=F32,
-    ).astype(BF16)
-    grad_all[my_col] = grad_own[...]
-
-    def grad_copy(k, src_index):
-        return to_col(grad_own, grad_all.at[src_index], gs.at[k], gr.at[src_index], col_peer(k))
-
-    each(n_col, lambda k: grad_copy(k, my_col).start())
-    update = jnp.dot(activated, wo2_ref[...], preferred_element_type=F32) + bo2_ref[...]
-    fout_ref[...] = (feat_ref[...].astype(F32) + jnp.transpose(update)).astype(BF16)
-    run(SPLIT, total_groups, derivative_group)
-    each(n_col, lambda k: grad_copy(k, col_peer(k)).wait_recv())
-
-    def spread_grad(s, carry):
-        t, _ = tiles_of(s)
-        grad_f[s] = grad_all[t].astype(F32)
-        return carry
-
-    lax.fori_loop(0, n_slot, spread_grad, 0)
+
+    def grad_copy(h, k, src_index):
+        return to_col(
+            grad_own.at[h], grad_all[h].at[src_index], gs.at[h * n_col + k],
+            gr.at[h * n_col + src_index], col_peer(k),
+        )
+
+    def atom_update(h):
+        each(n_col, lambda k: msg_copy(h, k, col_peer(k), col_peer(k)).wait_recv())
+        total = msg_in[h, 0].astype(F32)
+        for k in range(1, n_col):
+            total = total + msg_in[h, k].astype(F32)
+        act_in = jnp.dot(total.astype(BF16), wo1_ref[...], preferred_element_type=F32) + bo1_ref[...]
+        small = jnp.exp(-jnp.abs(act_in))
+        activated = (jnp.maximum(act_in, 0.0) + jnp.log(1.0 + small) - LN2).astype(BF16)
+        sig = jnp.where(act_in >= 0.0, 1.0, small) / (1.0 + small)
+        grad_own[h] = lax.dot_general(
+            sig * direction, wo1_ref[...].astype(F32), (((1,), (1,)), ((), ())),
+            precision=lax.Precision.HIGHEST, preferred_element_type=F32,
+        ).astype(BF16)
+        grad_all[h][my_col] = grad_own[h]
+        each(n_col, lambda k: grad_copy(h, k, my_col).start())
+        update[part_rows(h)] = (
+            jnp.dot(activated, wo2_ref[...], preferred_element_type=F32) + bo2_ref[...]
+        )
+
+    done = 0
+    for h in range(groups):
+        run(done, SPLITS[h], derivative_group)
+        done = SPLITS[h]
+        atom_update(h)
+    run(done, total_groups, derivative_group)
+    fout_ref[...] = (feat_ref[...].astype(F32) + jnp.transpose(update[...])).astype(BF16)
+
+    def spread_grad(h):
+        def body(s, carry):
+            t, _ = tiles_of(s)
+            grad_f[s, part_rows(h)] = grad_all[h][t].astype(F32)
+            return carry
+        lax.fori_loop(0, n_slot, body, 0)
 
     def dist_group(n):
-        s, base = n // groups, lax.rem(n, groups) * PAIRS
+        s, base = place(n)
         w2 = w2_ref[...]
         lhs = jnp.concatenate(
             [
                 jnp.concatenate(
                     [
-                        w2 * row16(grad_f[s, pl.ds(base + b, 1), :]),
-                        w2 * row16(grad_f[s, pl.ds(base + b + half, 1), :]),
+                        w2 * row16(grad_f[s, pl.ds(2 * base + b, 1), :]),
+                        w2 * row16(grad_f[s, pl.ds(2 * base + b + PAIRS, 1), :]),
                     ],
                     axis=1,
                 )
@@ -369,10 +424,13 @@
             product = q[b * 128:(b + 1) * 128].astype(BF16) * hid[s, base + b]
             folded = (product[0:64] + product[64:128]).astype(F32)
             row = jnp.sum(folded, axis=0, keepdims=True)
-            dgrad[s, pl.ds(base + b, 1), :] = row[:, 0:128]
-            dgrad[s, pl.ds(base + b + half, 1), :] = row[:, 128:256]
-
-    run(0, total_groups, dist_group)
+            dgrad[s, pl.ds(2 * base + b, 1), :] = row[:, 0:128]
+            dgrad[s, pl.ds(2 * base + b + PAIRS, 1), :] = row[:, 128:256]
+
+    for h in range(groups):
+        each(n_col, lambda k, h=h: grad_copy(h, k, col_peer(k)).wait_recv())
+        spread_grad(h)
+        run(h * n_slot, (h + 1) * n_slot, dist_group)
 
     def force_slot(s, carry):
         g_b2 = (grad_f[s] * b2_ref[...]).astype(BF16)
@@ -416,11 +474,13 @@
 
     each(n_row, lambda k: pos_col_copy(k, my_row).wait_send())
     each(n_col, lambda k: pos_row_copy(k, my_col).wait_send())
-    each(n_chip, lambda k: proj_copy(k, my_row).wait_send())
-    proj_hand(0).wait_send()
-    each(n_chip, lambda k: proj_hand(k).wait_send())
-    each(n_col, lambda k: msg_copy(k, col_peer(k), my_col).wait_send())
-    each(n_col, lambda k: grad_copy(k, my_col).wait_send())
+    each(n_ring, lambda k: ring_copy(k).wait_send())
+    every(n_ring, lambda k: twin_copy(k).wait_send())
+    every(n_ring, lambda k: hand_near(k).wait_send())
+    every(n_ring, lambda k: hand_far(k).wait_send())
+    for h in range(groups):
+        each(n_col, lambda k, h=h: msg_copy(h, k, col_peer(k), my_col).wait_send())
+        each(n_col, lambda k, h=h: grad_copy(h, k, my_col).wait_send())
 
     each(n_col, lambda k: rforce_copy(k, col_peer(k), col_peer(k)).wait_recv())
     each(n_row, lambda k: cforce_copy(k, row_peer(k), row_peer(k)).wait_recv())
@@ -469,10 +529,12 @@
                 pltpu.VMEM((n_slot, 64, 128, 256), BF16),
                 pltpu.VMEM((n_slot, 64, 64, 256), BF16),
                 pltpu.VMEM((n_slot,) + tile, F32),
-                pltpu.VMEM((n_col,) + tile, BF16),
-                pltpu.VMEM((n_col,) + tile, BF16),
-                pltpu.VMEM(tile, BF16),
-                pltpu.VMEM((n_col,) + tile, BF16),
+                pltpu.VMEM((64 // PAIRS, n_col, 2 * PAIRS, 128), BF16),
+                pltpu.VMEM((64 // PAIRS, n_col, 2 * PAIRS, 128), BF16),
+                pltpu.VMEM((64 // PAIRS, 2 * PAIRS, 128), BF16),
+                pltpu.VMEM((n_col, 2 * PAIRS, 128), BF16),
+                pltpu.VMEM((n_col, 2 * PAIRS, 128), BF16),
+                pltpu.VMEM(tile, F32),
                 pltpu.VMEM((n_slot,) + tile, F32),
                 pltpu.VMEM((n_slot,) + tile, F32),
                 pltpu.VMEM((n_slot, 8, 128), F32),
@@ -483,9 +545,9 @@
                 pltpu.VMEM((n_row, 3, 128), F32),
                 dma((n_row,)), dma((n_row,)),
                 dma((n_col,)), dma((n_col,)),
-                dma((n_row // 2,)), dma((n_row // 2,)), dma((n_row,)),
-                dma((n_col,)), dma((n_col,)),
-                dma((n_col,)), dma((n_col,)),
+                dma((n_row // 4,)), dma((n_row // 4,)), dma((n_row // 2,)), dma((n_row,)),
+                dma((64 // PAIRS * n_col,)), dma((64 // PAIRS * n_col,)),
+                dma((64 // PAIRS * n_col,)), dma((64 // PAIRS * n_col,)),
                 dma((n_col,)), dma((n_col,)),
                 dma((n_row,)), dma((n_row,)),
             ],

time: 72.9 us -> 69.9 us (0.959)
  Pallas kernels: 69.5 us -> 66.5 us
    pallas_call x1, Pallas kernels: 69.5 us -> 66.5 us  [local(): pl.pallas_call(functools.partial(kernel, n_row, n_col, n_slot), out_shape...]
where the time goes in v4:
time: 69.9 us; the launch traced here: 69.8 us
  Pallas kernels  66.5 us (95%)
  local copies, waits for them, and re-layouts  1.96 us (3%)
  between operations  1.3 us (2%)
    pallas_call x1, Pallas kernels, local(): pl.pallas_call(functools.partial(kernel, n_row, n_col, n_slot), out_shape...  66.5 us
    unnamed x4, local copies, waits for them, and re-layouts  1.96 us

profile of v4, /device:TPU:1, one launch (start us, length us, event | category | flops | bytes accessed | tf_op | source)
XLA Modules:
  0.0 69.8 jit_solution(13751832767029879279)
XLA Ops:
  1.3 66.5 %shard_map.158 = (bf16[128,128]{1,0:T(8,128)(2,1)}, f32[3,128]{1,0:T(4,128)}) custom-call(s32[2,4]{1,0:T(2,128)} %bitcast.8, s32[1,1]{1,0:T(1,128)S(6)} %copy.19.count_ref, bf16[128,128]{1,0:T(8,128)(2,1)} %feat_ref.1, f32[3,128]{1,0:T(4,128)} %pos_ref.1, s32[4,128,128]{2,1,0:T(8,128)} %bitcast.7, bf16[128,128]{1,0:T(8,128)(2,1)} %w_in_ref.1, ...), custom_call_target="tpu_custom_call" | custom-call | tf_op jit(solution)/shard_map/pallas_call | solution.py:507
  67.8 0.0 copy-start
  67.8 1.4 %copy.20 = bf16[128,128]{1,0:T(8,128)(2,1)} copy(bf16[128,128]{1,0:T(8,128)(2,1)} %get-tuple-element.4) | data formatting | bytes 65536
  69.2 0.0 copy-done
  69.2 0.6 copy.21
Async XLA Ops:
  67.8 1.4 %copy-start = (f32[3,128]{1,0:T(4,128)S(1)}, f32[3,128]{1,0:T(4,128)}, u32[]{:S(2)}) copy-start(f32[3,128]{1,0:T(4,128)} %get-tuple-element.5) | copy-start | bytes 4612

commit v5 on v4

--- a/solution.py
+++ b/solution.py
@@ -20,8 +20,8 @@
 MESH = pl.DeviceIdType.MESH
 PAIRS = 32
 PASS = 0
-HAND = 4
-LAG = 5
+HAND = 5
+LAG = 6
 SPLITS = (2, 5)
 
 

time: 69.9 us -> 70.4 us (level)
  no operation moved by 1% of the time
where the time goes in v5:
time: 70.4 us; the launch traced here: 70.2 us
  Pallas kernels  67 us (95%)
  local copies, waits for them, and re-layouts  1.96 us (3%)
  between operations  1.3 us (2%)
    pallas_call x1, Pallas kernels, local(): pl.pallas_call(functools.partial(kernel, n_row, n_col, n_slot), out_shape...  67 us
    unnamed x4, local copies, waits for them, and re-layouts  1.96 us

profile of v5, /device:TPU:1, one launch (start us, length us, event | category | flops | bytes accessed | tf_op | source)
XLA Modules:
  0.0 70.2 jit_solution(11484563081122582960)
XLA Ops:
  1.3 67.0 %shard_map.158 = (bf16[128,128]{1,0:T(8,128)(2,1)}, f32[3,128]{1,0:T(4,128)}) custom-call(s32[2,4]{1,0:T(2,128)} %bitcast.8, s32[1,1]{1,0:T(1,128)S(6)} %copy.19.count_ref, bf16[128,128]{1,0:T(8,128)(2,1)} %feat_ref.1, f32[3,128]{1,0:T(4,128)} %pos_ref.1, s32[4,128,128]{2,1,0:T(8,128)} %bitcast.7, bf16[128,128]{1,0:T(8,128)(2,1)} %w_in_ref.1, ...), custom_call_target="tpu_custom_call" | custom-call | tf_op jit(solution)/shard_map/pallas_call | solution.py:507
  68.3 0.0 copy-start
  68.3 1.4 %copy.20 = bf16[128,128]{1,0:T(8,128)(2,1)} copy(bf16[128,128]{1,0:T(8,128)(2,1)} %get-tuple-element.4) | data formatting | bytes 65536
  69.7 0.0 copy-done
  69.7 0.6 copy.21
Async XLA Ops:
  68.3 1.4 %copy-start = (f32[3,128]{1,0:T(4,128)S(1)}, f32[3,128]{1,0:T(4,128)}, u32[]{:S(2)}) copy-start(f32[3,128]{1,0:T(4,128)} %get-tuple-element.5) | copy-start | bytes 4612
